TPU v7x, 32 devices: a whole 2x2x4 slice. The times are simulated.
32 devices in a mesh: chain: 4 (over x, core), col: 8 (over z, y).
Axes of the slice: x: 2, y: 2, z: 4, core: 2. Of those that a mesh axis runs over, the one named last changes fastest.
Arguments:
- rhs: float32 [4, 8, 64, 128], P('chain', 'col'), may hold values from -6 to 6
- inverse: float32 [4, 8, 128, 128], P('chain', 'col'), as said below
- factor: float32 [4, 8, 8, 128, 128], P('chain', 'col'), may hold values from -0.1875 to 0.1875
- pattern: int32 [4, 8, 8], P('chain', 'col'), may hold values from 0 to 7, as said below
Outputs:
- forward: float32 [4, 8, 64, 128], P('chain', 'col')
- solution: float32 [4, 8, 64, 128], P('chain', 'col')
Inputs may be any that keep to these rules, and one draw needn't show every extreme that they name: `pattern`: the 8 block rows of one supernode are distinct. `inverse`: each block is lower triangular, its diagonal between 0.5 and 1.5.
All inputs are finite; a program needn't handle non-finite values.
Results may differ from a plain program's by a relative error of at most 0.00012.
Values sent between devices are 32-bit elements; how exact they have to be, the bound alone decides.
A program may use at most 64 MiB of HBM per device.

v0:
```python
import jax
import jax.numpy as jnp
from jax import lax
from jax.sharding import PartitionSpec as P


def shifted(value, axis, steps):
    count = lax.axis_size(axis)
    first, last = (max(0, -steps), min(count, count - steps))
    return lax.ppermute(value, axis, [(source, source + steps) for source in range(first, last)])


def body(rhs, inverse, factor, pattern):
    levels = lax.axis_size("chain")
    supers = lax.axis_size("col")
    highest = lax.Precision.HIGHEST
    loads_block = rhs[0, 0]
    diag_inverse = inverse[0, 0]
    blocks = factor[0, 0]
    targets = pattern[0, 0]
    loads, width = loads_block.shape
    place = lax.axis_index("chain")
    onehot = (targets[:, None] == jnp.arange(supers, dtype=jnp.int32)[None, :]).astype(jnp.float32)
    pieces = 1
    rows = loads // pieces
    steps = levels + pieces - 1

    def window(step, lag):
        index = step - lag
        live = (index >= 0) & (index < pieces)
        start = jnp.clip(index, 0, pieces - 1) * rows
        return (live, start)

    def forward_step(step, carry):
        solved, incoming = carry
        live, start = window(step, place)
        residue = loads_block - incoming
        fresh = jnp.dot(residue, diag_inverse.T, precision=highest)
        solved = jnp.where(live, fresh, solved)
        terms = jnp.einsum("rb,kab->kra", fresh, blocks, precision=highest)
        spread = jnp.einsum("kc,kra->cra", onehot, terms, precision=highest)
        received = lax.all_to_all(spread, "col", split_axis=0, concat_axis=0, tiled=True)
        summed_rows = jnp.sum(received, axis=0)
        arrived = shifted(summed_rows, "chain", 1)
        got, into = window(step + 1, place)
        got = got & (place > 0)
        incoming = jnp.where(got, arrived, incoming)
        return (solved, incoming)

    empty = jnp.zeros((loads, width), jnp.float32)
    solved, unused = lax.fori_loop(0, steps, forward_step, (empty, empty))

    def backward_step(step, carry):
        answer, outgoing = carry
        lag = levels - 1 - place
        live, start = window(step, lag)
        residue = solved - outgoing
        fresh = jnp.dot(residue, diag_inverse, precision=highest)
        answer = jnp.where(live, fresh, answer)
        arrived = shifted(fresh, "chain", -1)
        picked = jnp.einsum(
            "kc,cra->kra",
            onehot,
            lax.all_gather(arrived[None], "col", axis=0, tiled=True),
            precision=highest,
        )
        term = jnp.einsum("kra,kab->rb", picked, blocks, precision=highest)
        got, into = window(step, lag - 1)
        got = got & (place < levels - 1)
        outgoing = jnp.where(got, term, outgoing)
        return (answer, outgoing)

    answer, unused_rows = lax.fori_loop(0, steps, backward_step, (empty, empty))
    return (solved[None, None], answer[None, None])


def solution(mesh):
    in_specs = (
        P("chain", "col", None, None),
        P("chain", "col", None, None),
        P("chain", "col", None, None, None),
        P("chain", "col", None),
    )
    out_specs = (P("chain", "col", None, None), P("chain", "col", None, None))
    return jax.shard_map(body, mesh=mesh, in_specs=in_specs, out_specs=out_specs, check_vma=False)
```

profile of v0, /device:TPU:0, one launch (start us, length us, event | category | flops | bytes accessed | tf_op | source)
XLA Modules:
  0.0 229.1 jit_solution(17042671163509285255)
XLA Ops:
  1.3 80.9 %while.35 = (s32[]{:T(128)}, f32[64,128]{1,0:T(8,128)S(1)}, f32[64,128]{1,0:T(8,128)S(1)}, s32[]{:T(128)}, f32[64,128]{1,0:T(8,128)}, /*index=5*/f32[128,128]{1,...) while((s32[]{:T(128)}, f32[64,128]{1,0:T(8,128)S(1)}, ...), condition=%wide.region_2.3_spmd.clone, body=%wide.region_0.2_spmd.clone.sunk | while | flops 119644296 | bytes 3146003 | solution.py:51
  1.3 1.1 select_select_fusion.6
  2.4 1.7 fusion.53
  4.7 16.0 %all_to_all.12 = f32[8,64,128]{2,1,0:T(8,128)S(1)} all-to-all(f32[8,64,128]{2,1,0:T(8,128)S(1)} %copy.25), channel_id=1, replica_groups=mesh['chain'=4,'col'=8] {'col'}, dimensions={0} | all-to-all | bytes 524288 | tf_op jit(solution)/shard_map/while/body/eval_jaxpr/all_to_all | solution.py:42
  20.8 1.3 collective-permute-start
  22.9 1.1 select_select_fusion.6
  24.0 1.7 fusion.53
  26.3 12.4 %all_to_all.12 = f32[8,64,128]{2,1,0:T(8,128)S(1)} all-to-all(f32[8,64,128]{2,1,0:T(8,128)S(1)} %copy.25), channel_id=1, replica_groups=mesh['chain'=4,'col'=8] {'col'}, dimensions={0} | all-to-all | bytes 524288 | tf_op jit(solution)/shard_map/while/body/eval_jaxpr/all_to_all | solution.py:42
  38.7 3.1 %collective-permute-start = (f32[64,128]{1,0:T(8,128)S(1)}, f32[64,128]{1,0:T(8,128)S(1)}, u32[]{:S(2)}, u32[]{:S(2)}) collective-permute-start(f32[64,128]{1,0:T(8,128)S(1)} %reduce_sum.16), channel_id=1, source_target_pairs={{0,8},{8,16},{16,24},{1,9},{9,17},{17,25},{2,10},{10,18},{18,26},{... | collective-permute-start | bytes 98312 | tf_op jit(solution)/shard_map/while/body/eval_jaxpr/ppermute | solution.py:10
  42.7 1.1 select_select_fusion.6
  43.8 1.7 fusion.53
  46.1 12.5 %all_to_all.12 = f32[8,64,128]{2,1,0:T(8,128)S(1)} all-to-all(f32[8,64,128]{2,1,0:T(8,128)S(1)} %copy.25), channel_id=1, replica_groups=mesh['chain'=4,'col'=8] {'col'}, dimensions={0} | all-to-all | bytes 524288 | tf_op jit(solution)/shard_map/while/body/eval_jaxpr/all_to_all | solution.py:42
  58.6 3.0 %collective-permute-start = (f32[64,128]{1,0:T(8,128)S(1)}, f32[64,128]{1,0:T(8,128)S(1)}, u32[]{:S(2)}, u32[]{:S(2)}) collective-permute-start(f32[64,128]{1,0:T(8,128)S(1)} %reduce_sum.16), channel_id=1, source_target_pairs={{0,8},{8,16},{16,24},{1,9},{9,17},{17,25},{2,10},{10,18},{18,26},{... | collective-permute-start | bytes 98312 | tf_op jit(solution)/shard_map/while/body/eval_jaxpr/ppermute | solution.py:10
  62.4 1.1 select_select_fusion.6
  63.5 1.7 fusion.53
  65.8 12.9 %all_to_all.12 = f32[8,64,128]{2,1,0:T(8,128)S(1)} all-to-all(f32[8,64,128]{2,1,0:T(8,128)S(1)} %copy.25), channel_id=1, replica_groups=mesh['chain'=4,'col'=8] {'col'}, dimensions={0} | all-to-all | bytes 524288 | tf_op jit(solution)/shard_map/while/body/eval_jaxpr/all_to_all | solution.py:42
  78.7 2.7 %collective-permute-start = (f32[64,128]{1,0:T(8,128)S(1)}, f32[64,128]{1,0:T(8,128)S(1)}, u32[]{:S(2)}, u32[]{:S(2)}) collective-permute-start(f32[64,128]{1,0:T(8,128)S(1)} %reduce_sum.16), channel_id=1, source_target_pairs={{0,8},{8,16},{16,24},{1,9},{9,17},{17,25},{2,10},{10,18},{18,26},{... | collective-permute-start | bytes 98312 | tf_op jit(solution)/shard_map/while/body/eval_jaxpr/ppermute | solution.py:10
  82.3 146.2 %while.36 = (s32[]{:T(128)}, f32[64,128]{1,0:T(8,128)S(1)}, f32[64,128]{1,0:T(8,128)S(1)}, s32[]{:T(128)}, f32[64,128]{1,0:T(8,128)S(1)}, /*index=5*/f32[128,128...) while((s32[]{:T(128)}, f32[64,128]{1,0:T(8,128)S(1)}, ...), condition=%wide.region_4.5_spmd.clone, body=%wide.region_3.4_spmd.clone.sunk | while | flops 119586952 | bytes 4129067 | solution.py:73
  82.3 1.1 select_select_fusion.8
  83.4 1.3 collective-permute-start.1
  84.7 3.7 %collective-permute-done.1 = f32[64,128]{1,0:T(8,128)S(1)} collective-permute-done((f32[64,128]{1,0:T(8,128)S(1)}, f32[64,128]{1,0:T(8,128)S(1)}, u32[]{:S(2)}, u32[]{:S(2)}) %collective-permute-start.1) | collective-permute-done | bytes 32800 | tf_op jit(solution)/shard_map/while/body/eval_jaxpr/ppermute | solution.py:10
  88.4 30.7 %all-gather.3 = f32[512,128]{1,0:T(8,128)S(1)} all-gather(f32[64,128]{1,0:T(8,128)S(1)} %collective-permute-done.1), channel_id=2, replica_groups=mesh['chain'=4,'col'=8] {'col'}, dimensions={0}, use_global_device_ids=true | all-gather | bytes 294912 | tf_op jit(solution)/shard_map/while/body/eval_jaxpr/all_gather | solution.py:64
  120.2 1.1 select_select_fusion.8
  121.3 1.3 collective-permute-start.1
  122.6 1.8 collective-permute-done.1
  124.4 31.0 %all-gather.3 = f32[512,128]{1,0:T(8,128)S(1)} all-gather(f32[64,128]{1,0:T(8,128)S(1)} %collective-permute-done.1), channel_id=2, replica_groups=mesh['chain'=4,'col'=8] {'col'}, dimensions={0}, use_global_device_ids=true | all-gather | bytes 294912 | tf_op jit(solution)/shard_map/while/body/eval_jaxpr/all_gather | solution.py:64
  157.6 1.3 collective-permute-start.1
  158.9 1.8 collective-permute-done.1
  160.7 30.8 %all-gather.3 = f32[512,128]{1,0:T(8,128)S(1)} all-gather(f32[64,128]{1,0:T(8,128)S(1)} %collective-permute-done.1), channel_id=2, replica_groups=mesh['chain'=4,'col'=8] {'col'}, dimensions={0}, use_global_device_ids=true | all-gather | bytes 294912 | tf_op jit(solution)/shard_map/while/body/eval_jaxpr/all_gather | solution.py:64
  193.6 1.3 collective-permute-start.1
  194.9 1.8 collective-permute-done.1
  196.7 30.8 %all-gather.3 = f32[512,128]{1,0:T(8,128)S(1)} all-gather(f32[64,128]{1,0:T(8,128)S(1)} %collective-permute-done.1), channel_id=2, replica_groups=mesh['chain'=4,'col'=8] {'col'}, dimensions={0}, use_global_device_ids=true | all-gather | bytes 294912 | tf_op jit(solution)/shard_map/while/body/eval_jaxpr/all_gather | solution.py:64
  (48 shorter events, 13.0 us)
Async XLA Ops:
  0.7 0.7 copy-start.3
  20.8 2.1 collective-permute-start
  38.7 4.0 %collective-permute-start = (f32[64,128]{1,0:T(8,128)S(1)}, f32[64,128]{1,0:T(8,128)S(1)}, u32[]{:S(2)}, u32[]{:S(2)}) collective-permute-start(f32[64,128]{1,0:T(8,128)S(1)} %reduce_sum.16), channel_id=1, source_target_pairs={{0,8},{8,16},{16,24},{1,9},{9,17},{17,25},{2,10},{10,18},{18,26},{... | collective-permute-start | bytes 98312 | tf_op jit(solution)/shard_map/while/body/eval_jaxpr/ppermute | solution.py:10
  58.6 3.8 %collective-permute-start = (f32[64,128]{1,0:T(8,128)S(1)}, f32[64,128]{1,0:T(8,128)S(1)}, u32[]{:S(2)}, u32[]{:S(2)}) collective-permute-start(f32[64,128]{1,0:T(8,128)S(1)} %reduce_sum.16), channel_id=1, source_target_pairs={{0,8},{8,16},{16,24},{1,9},{9,17},{17,25},{2,10},{10,18},{18,26},{... | collective-permute-start | bytes 98312 | tf_op jit(solution)/shard_map/while/body/eval_jaxpr/ppermute | solution.py:10
  78.7 3.5 %collective-permute-start = (f32[64,128]{1,0:T(8,128)S(1)}, f32[64,128]{1,0:T(8,128)S(1)}, u32[]{:S(2)}, u32[]{:S(2)}) collective-permute-start(f32[64,128]{1,0:T(8,128)S(1)} %reduce_sum.16), channel_id=1, source_target_pairs={{0,8},{8,16},{16,24},{1,9},{9,17},{17,25},{2,10},{10,18},{18,26},{... | collective-permute-start | bytes 98312 | tf_op jit(solution)/shard_map/while/body/eval_jaxpr/ppermute | solution.py:10
  82.3 37.4 %copy-start = (f32[8,128,128]{2,1,0:T(8,128)S(1)}, f32[8,128,128]{2,1,0:T(8,128)}, u32[]{:S(2)}) copy-start(f32[8,128,128]{2,1,0:T(8,128)} %get-tuple-element.685) | copy-start | bytes 1572868 | tf_op jit(solution)/shard_map/while
  83.4 5.0 %collective-permute-start.1 = (f32[64,128]{1,0:T(8,128)S(1)}, f32[64,128]{1,0:T(8,128)S(1)}, u32[]{:S(2)}, u32[]{:S(2)}) collective-permute-start(f32[64,128]{1,0:T(8,128)S(1)} %get-tuple-element.616), channel_id=1, source_target_pairs={{8,0},{16,8},{24,16},{9,1},{17,9},{25,17},{10,2},{18,10},{26,18},{... | collective-permute-start | bytes 98312 | tf_op jit(solution)/shard_map/while/body/eval_jaxpr/ppermute | solution.py:10
  120.2 35.8 %copy-start = (f32[8,128,128]{2,1,0:T(8,128)S(1)}, f32[8,128,128]{2,1,0:T(8,128)}, u32[]{:S(2)}) copy-start(f32[8,128,128]{2,1,0:T(8,128)} %get-tuple-element.685) | copy-start | bytes 1572868 | tf_op jit(solution)/shard_map/while
  121.3 3.1 %collective-permute-start.1 = (f32[64,128]{1,0:T(8,128)S(1)}, f32[64,128]{1,0:T(8,128)S(1)}, u32[]{:S(2)}, u32[]{:S(2)}) collective-permute-start(f32[64,128]{1,0:T(8,128)S(1)} %get-tuple-element.616), channel_id=1, source_target_pairs={{8,0},{16,8},{24,16},{9,1},{17,9},{25,17},{10,2},{18,10},{26,18},{... | collective-permute-start | bytes 98312 | tf_op jit(solution)/shard_map/while/body/eval_jaxpr/ppermute | solution.py:10
  156.5 35.5 %copy-start = (f32[8,128,128]{2,1,0:T(8,128)S(1)}, f32[8,128,128]{2,1,0:T(8,128)}, u32[]{:S(2)}) copy-start(f32[8,128,128]{2,1,0:T(8,128)} %get-tuple-element.685) | copy-start | bytes 1572868 | tf_op jit(solution)/shard_map/while
  157.6 3.1 %collective-permute-start.1 = (f32[64,128]{1,0:T(8,128)S(1)}, f32[64,128]{1,0:T(8,128)S(1)}, u32[]{:S(2)}, u32[]{:S(2)}) collective-permute-start(f32[64,128]{1,0:T(8,128)S(1)} %get-tuple-element.616), channel_id=1, source_target_pairs={{8,0},{16,8},{24,16},{9,1},{17,9},{25,17},{10,2},{18,10},{26,18},{... | collective-permute-start | bytes 98312 | tf_op jit(solution)/shard_map/while/body/eval_jaxpr/ppermute | solution.py:10
  192.5 35.5 %copy-start = (f32[8,128,128]{2,1,0:T(8,128)S(1)}, f32[8,128,128]{2,1,0:T(8,128)}, u32[]{:S(2)}) copy-start(f32[8,128,128]{2,1,0:T(8,128)} %get-tuple-element.685) | copy-start | bytes 1572868 | tf_op jit(solution)/shard_map/while
  193.6 3.1 %collective-permute-start.1 = (f32[64,128]{1,0:T(8,128)S(1)}, f32[64,128]{1,0:T(8,128)S(1)}, u32[]{:S(2)}, u32[]{:S(2)}) collective-permute-start(f32[64,128]{1,0:T(8,128)S(1)} %get-tuple-element.616), channel_id=1, source_target_pairs={{8,0},{16,8},{24,16},{9,1},{17,9},{25,17},{10,2},{18,10},{26,18},{... | collective-permute-start | bytes 98312 | tf_op jit(solution)/shard_map/while/body/eval_jaxpr/ppermute | solution.py:10
  228.5 0.6 copy-start.1
  228.5 0.6 copy-start.2
where the time goes:
time: 231 us; the launch traced here: 229 us
  blocking collectives  177 us (77%)
  matrix products  21.5 us (9%)
  starting transfers between devices  15.2 us (7%)
  waiting for transfers between devices  12.4 us (5%)
    all_gather x4, blocking collectives, backward_step(): lax.all_gather(arrived[None], 'col', axis=0, tiled=True)  123 us
    all_to_all x4, blocking collectives, forward_step(): lax.all_to_all(spread, 'col', split_axis=0, concat_axis=0, tiled=True)  53.8 us
    ppermute x8, starting transfers between devices, shifted(): lax.ppermute(value, axis, [(source, source + steps) for source in range(f...  15.2 us
    ppermute x8, waiting for transfers between devices, shifted(): lax.ppermute(value, axis, [(source, source + steps) for source in range(f...  12.4 us
    dot_general x4, matrix products, forward_step(): terms = jnp.einsum('rb,kab->kra', fresh, blocks, precision=highest)  6.82 us
  transfers between devices with their start and end apart: 8, of which 8 were waited for; matrix products, arithmetic and copies ran while one was open for 0% of the time, Pallas kernels for 0%

commit v1 on v0

v1 whole, which is shorter than its diff:
```python
import functools

import jax
import jax.numpy as jnp
from jax import lax
from jax.experimental import pallas as pl
from jax.experimental.pallas import tpu as pltpu
from jax.sharding import PartitionSpec as P

PIECES = 2
MESH = pl.DeviceIdType.MESH


def halves(value):
    high = value.astype(jnp.bfloat16)
    low = (value - high.astype(jnp.float32)).astype(jnp.bfloat16)
    return high, low


def times_transposed(value, packed):
    rows = value.shape[0]
    high, low = halves(value)
    stacked = jnp.concatenate(
        [jnp.concatenate([high, low], axis=1), jnp.concatenate([low, high], axis=1)], axis=0
    )
    both = lax.dot_general(
        stacked, packed, (((1,), (1,)), ((), ())), preferred_element_type=jnp.float32
    )
    return both[:rows] + both[rows:]


def times(value, packed):
    rows = value.shape[0]
    width = packed.shape[1] // 2
    high, low = halves(value)
    both = jnp.dot(
        jnp.concatenate([high, low], axis=0), packed, preferred_element_type=jnp.float32
    )
    summed = both[:rows] + both[rows:]
    return summed[:, :width] + summed[:, width:]


def kernel(
    levels, supers, rhs_hbm, inverse_hbm, factor_hbm, pattern_hbm, forward_ref, answer_ref,
    rhs, inverse, factor, pattern, inverse_packed, factor_packed, terms, outbox, inbox, solved,
    load_sem, outbox_sem, inbox_sem, solved_sem, arrived_sem, *arrived,
):
    place = lax.axis_index("chain")
    me = lax.axis_index("col")
    count, _, width = factor.shape
    loads = rhs.shape[0]
    rows = loads // PIECES
    loading = [
        pltpu.make_async_copy(source, target, load_sem.at[at])
        for at, (source, target) in enumerate(
            ((rhs_hbm, rhs), (inverse_hbm, inverse), (factor_hbm, factor), (pattern_hbm, pattern))
        )
    ]
    for copy in loading:
        copy.start()
    peers = [lax.rem(me + shift, supers) for shift in range(supers)]

    barrier = pltpu.get_barrier_semaphore()

    @pl.when(place > 0)
    def _():
        for peer in peers:
            pl.semaphore_signal(
                barrier, inc=1, device_id={"chain": place - 1, "col": peer}, device_id_type=MESH
            )

    @pl.when(place < levels - 1)
    def _():
        for peer in peers:
            pl.semaphore_signal(
                barrier, inc=1, device_id={"chain": place + 1, "col": peer}, device_id_type=MESH
            )

    loading[0].wait()
    loading[1].wait()
    high, low = halves(inverse[...])
    inverse_packed[:, :width] = high
    inverse_packed[:, width:] = low
    loading[2].wait()
    for block in range(count):
        high, low = halves(factor[block])
        factor_packed[block * width:(block + 1) * width, :width] = high
        factor_packed[block * width:(block + 1) * width, width:] = low
    loading[3].wait()
    targets = [pattern[0, 0, block] for block in range(count)]
    origin = []
    for peer in peers:
        at = jnp.int32(-1)
        for block in range(count):
            at = jnp.where(targets[block] == peer, jnp.int32(block), at)
        origin.append(at)
    slots = [lax.rem(me - target + supers, supers) for target in targets]

    pl.semaphore_wait(
        barrier, jnp.where(place > 0, supers, 0) + jnp.where(place < levels - 1, supers, 0)
    )

    def term_copy(piece, shift):
        return pltpu.make_async_remote_copy(
            src_ref=outbox.at[piece, shift],
            dst_ref=inbox.at[piece, shift],
            send_sem=outbox_sem.at[piece, shift],
            recv_sem=inbox_sem.at[piece, shift],
            device_id={"chain": place + 1, "col": peers[shift]},
            device_id_type=MESH,
        )

    def answer_copy(piece, shift):
        return pltpu.make_async_remote_copy(
            src_ref=solved.at[piece],
            dst_ref=arrived[piece].at[shift],
            send_sem=solved_sem.at[piece, shift],
            recv_sem=arrived_sem.at[piece, shift],
            device_id={"chain": place - 1, "col": peers[shift]},
            device_id_type=MESH,
        )

    for piece in range(PIECES):
        part = pl.ds(piece * rows, rows)

        @pl.when(place > 0)
        def _():
            total = rhs[part, :]
            for shift in range(supers):
                pltpu.make_async_copy(
                    inbox.at[piece, shift], inbox.at[piece, shift], inbox_sem.at[piece, shift]
                ).wait()
                total = total - inbox[piece, shift]
            rhs[part, :] = total

        fresh = times_transposed(rhs[part, :], inverse_packed[...])
        forward_ref[part, :] = fresh

        @pl.when(place < levels - 1)
        def _():
            wide = times_transposed(fresh, factor_packed[...])
            for block in range(count):
                terms[block] = wide[:, block * width:(block + 1) * width]
            for shift in range(supers):
                picked = terms[jnp.maximum(origin[shift], 0)]
                if count < supers:
                    picked = jnp.where(origin[shift] >= 0, picked, 0.0)
                outbox[piece, shift] = picked
                term_copy(piece, shift).start()

    for piece in range(PIECES):
        part = pl.ds(piece * rows, rows)
        rhs[part, :] = forward_ref[part, :]

        @pl.when(place < levels - 1)
        def _():
            for shift in range(supers):
                pltpu.make_async_copy(
                    arrived[piece].at[shift], arrived[piece].at[shift], arrived_sem.at[piece, shift]
                ).wait()
            picked = jnp.concatenate([arrived[piece][slot] for slot in slots], axis=1)
            rhs[part, :] = rhs[part, :] - times(picked, factor_packed[...])

        fresh = times(rhs[part, :], inverse_packed[...])
        solved[piece] = fresh
        answer_ref[part, :] = fresh

        @pl.when(place > 0)
        def _():
            for shift in range(supers):
                answer_copy(piece, shift).start()

    @pl.when(place < levels - 1)
    def _():
        for piece in range(PIECES):
            for shift in range(supers):
                term_copy(piece, shift).wait_send()

    @pl.when(place > 0)
    def _():
        for piece in range(PIECES):
            for shift in range(supers):
                answer_copy(piece, shift).wait_send()


def body(rhs, inverse, factor, pattern):
    levels = lax.axis_size("chain")
    supers = lax.axis_size("col")
    loads, width = rhs.shape[2:]
    count = factor.shape[2]
    rows = loads // PIECES
    block = jax.ShapeDtypeStruct((loads, width), jnp.float32)
    anywhere = pl.BlockSpec(memory_space=pl.ANY)
    solved, answer = pl.pallas_call(
        functools.partial(kernel, levels, supers),
        out_shape=(block, block),
        in_specs=[anywhere] * 4,
        out_specs=[pl.BlockSpec(memory_space=pltpu.VMEM)] * 2,
        scratch_shapes=[
            pltpu.VMEM((loads, width), jnp.float32),
            pltpu.VMEM((width, width), jnp.float32),
            pltpu.VMEM((count, width, width), jnp.float32),
            pltpu.SMEM((1, 1, count), jnp.int32),
            pltpu.VMEM((width, 2 * width), jnp.bfloat16),
            pltpu.VMEM((count * width, 2 * width), jnp.bfloat16),
            pltpu.VMEM((count, rows, width), jnp.float32),
            pltpu.VMEM((PIECES, supers, rows, width), jnp.float32),
            pltpu.VMEM((PIECES, supers, rows, width), jnp.float32),
            pltpu.VMEM((PIECES, rows, width), jnp.float32),
            pltpu.SemaphoreType.DMA((4,)),
            pltpu.SemaphoreType.DMA((PIECES, supers)),
            pltpu.SemaphoreType.DMA((PIECES, supers)),
            pltpu.SemaphoreType.DMA((PIECES, supers)),
            pltpu.SemaphoreType.DMA((PIECES, supers)),
            *[pltpu.VMEM((supers, rows, width), jnp.float32)] * PIECES,
        ],
        compiler_params=pltpu.CompilerParams(collective_id=0, has_side_effects=True),
    )(rhs[0, 0], inverse[0, 0], factor[0, 0], pattern)
    return (solved[None, None], answer[None, None])


def solution(mesh):
    in_specs = (
        P("chain", "col", None, None),
        P("chain", "col", None, None),
        P("chain", "col", None, None, None),
        P("chain", "col", None),
    )
    out_specs = (P("chain", "col", None, None), P("chain", "col", None, None))
    return jax.shard_map(body, mesh=mesh, in_specs=in_specs, out_specs=out_specs, check_vma=False)
```

time: 231 us -> 40.7 us (0.18)
  blocking collectives: 177 us -> 0 us
  Pallas kernels: 0 us -> 37.9 us
  matrix products: 21.5 us -> 0 us
  starting transfers between devices: 15.2 us -> 0 us
  waiting for transfers between devices: 12.4 us -> 0 us
    all_gather x4 -> x0, blocking collectives: 123 us -> none  [backward_step(): lax.all_gather(arrived[None], 'col', axis=0, tiled=True)]
    all_to_all x4 -> x0, blocking collectives: 53.8 us -> none  [forward_step(): lax.all_to_all(spread, 'col', split_axis=0, concat_axis=0, tiled=True)]
    pallas_call x0 -> x1, Pallas kernels: none -> 37.9 us  [body(): pl.pallas_call(functools.partial(kernel, levels, supers), out_shape=(bloc...]
    dot_general x24 -> x0, matrix products: 21.5 us -> none  [the longest x4 6.82 us: forward_step(): terms = jnp.einsum('rb,kab->kra', fresh, blocks, precision=highest)]
    ppermute x8 -> x0, starting transfers between devices: 15.2 us -> none  [shifted(): lax.ppermute(value, axis, [(source, source + steps) for source in range(f...]
    ppermute x8 -> x0, waiting for transfers between devices: 12.4 us -> none  [shifted(): lax.ppermute(value, axis, [(source, source + steps) for source in range(f...]
  transfers between devices with their start and end apart: 8 -> 0, of which waited for: 8 -> 0; matrix products, arithmetic and copies ran while one was open for 0% -> 0% of each run, Pallas kernels for 0% -> 0%
where the time goes in v1:
time: 40.7 us; the launch traced here: 40.5 us
  Pallas kernels  37.9 us (93%)
  local copies, waits for them, and re-layouts  2 us (5%)
  between operations  0.65 us (2%)
    pallas_call x1, Pallas kernels, body(): pl.pallas_call(functools.partial(kernel, levels, supers), out_shape=(bloc...  37.9 us
    unnamed x4, local copies, waits for them, and re-layouts  2 us

profile of v1, /device:TPU:0, one launch (start us, length us, event | category | flops | bytes accessed | tf_op | source)
XLA Modules:
  0.0 40.5 jit_solution(5783529242645732455)
XLA Ops:
  0.6 37.9 %shard_map.59 = (f32[64,128]{1,0:T(8,128)}, f32[64,128]{1,0:T(8,128)}) custom-call(f32[64,128]{1,0:T(8,128)} %bitcast.7, f32[128,128]{1,0:T(8,128)} %bitcast.6, f32[8,128,128]{2,1,0:T(8,128)} %bitcast.5, s32[1,1,8]{2,1,0:T(1,128)} %pattern_hbm.1), custom_call_target="tpu_custom_call" | custom-call | tf_op jit(solution)/shard_map/pallas_call | solution.py:194
  38.5 0.0 copy-start
  38.5 1.4 %copy.8 = f32[1,1,64,128]{3,2,1,0:T(8,128)} copy(f32[1,1,64,128]{3,2,1,0:T(8,128)} %bitcast.9) | data formatting | bytes 65536
  39.9 0.0 copy-done
  39.9 0.6 %copy.9 = f32[1,1,64,128]{3,2,1,0:T(8,128)} copy(f32[1,1,64,128]{3,2,1,0:T(8,128)S(1)} %bitcast.8) | data formatting | bytes 65536
Async XLA Ops:
  38.5 1.4 %copy-start = (f32[64,128]{1,0:T(8,128)S(1)}, f32[64,128]{1,0:T(8,128)}, u32[]{:S(2)}) copy-start(f32[64,128]{1,0:T(8,128)} %get-tuple-element.5) | copy-start | bytes 98308

commit v2 on v1

--- a/solution.py
+++ b/solution.py
@@ -7,7 +7,7 @@
 from jax.experimental.pallas import tpu as pltpu
 from jax.sharding import PartitionSpec as P
 
-PIECES = 2
+PIECES = 4
 MESH = pl.DeviceIdType.MESH
 
 
@@ -42,7 +42,7 @@
 
 def kernel(
     levels, supers, rhs_hbm, inverse_hbm, factor_hbm, pattern_hbm, forward_ref, answer_ref,
-    rhs, inverse, factor, pattern, inverse_packed, factor_packed, terms, outbox, inbox, solved,
+    rhs, inverse, factor, pattern, inverse_packed, packed, terms, outbox, inbox, solved,
     load_sem, outbox_sem, inbox_sem, solved_sem, arrived_sem, *arrived,
 ):
     place = lax.axis_index("chain")
@@ -81,11 +81,17 @@
     high, low = halves(inverse[...])
     inverse_packed[:, :width] = high
     inverse_packed[:, width:] = low
+
+    def pack(block, value):
+        high, low = halves(value)
+        packed[block * width:(block + 1) * width, :width] = high
+        packed[block * width:(block + 1) * width, width:] = low
+
+    def pack_products():
+        for block in range(count):
+            pack(block, times(factor[block], inverse_packed[...]))
+
     loading[2].wait()
-    for block in range(count):
-        high, low = halves(factor[block])
-        factor_packed[block * width:(block + 1) * width, :width] = high
-        factor_packed[block * width:(block + 1) * width, width:] = low
     loading[3].wait()
     targets = [pattern[0, 0, block] for block in range(count)]
     origin = []
@@ -96,9 +102,20 @@
         origin.append(at)
     slots = [lax.rem(me - target + supers, supers) for target in targets]
 
-    pl.semaphore_wait(
-        barrier, jnp.where(place > 0, supers, 0) + jnp.where(place < levels - 1, supers, 0)
-    )
+    @pl.when(place == 0)
+    def _():
+        for block in range(count):
+            pack(block, factor[block])
+        rhs[...] = times_transposed(rhs[...], inverse_packed[...])
+        forward_ref[...] = rhs[...]
+
+    @pl.when((place > 0) & (place < levels - 1))
+    def _():
+        pack_products()
+
+    @pl.when(place == levels - 1)
+    def _():
+        pack(0, times(inverse[...].T, inverse_packed[...]))
 
     def term_copy(piece, shift):
         return pltpu.make_async_remote_copy(
@@ -133,12 +150,9 @@
                 total = total - inbox[piece, shift]
             rhs[part, :] = total
 
-        fresh = times_transposed(rhs[part, :], inverse_packed[...])
-        forward_ref[part, :] = fresh
-
         @pl.when(place < levels - 1)
         def _():
-            wide = times_transposed(fresh, factor_packed[...])
+            wide = times_transposed(rhs[part, :], packed[...])
             for block in range(count):
                 terms[block] = wide[:, block * width:(block + 1) * width]
             for shift in range(supers):
@@ -146,29 +160,54 @@
                 if count < supers:
                     picked = jnp.where(origin[shift] >= 0, picked, 0.0)
                 outbox[piece, shift] = picked
+
+        @pl.when(place == levels - 1)
+        def _():
+            fresh = times(rhs[part, :], packed[:width, :])
+            solved[piece] = fresh
+            answer_ref[part, :] = fresh
+
+        if piece == 0:
+            pl.semaphore_wait(
+                barrier, jnp.where(place > 0, supers, 0) + jnp.where(place < levels - 1, supers, 0)
+            )
+
+        @pl.when(place < levels - 1)
+        def _():
+            for shift in range(supers):
                 term_copy(piece, shift).start()
 
-    for piece in range(PIECES):
-        part = pl.ds(piece * rows, rows)
-        rhs[part, :] = forward_ref[part, :]
-
-        @pl.when(place < levels - 1)
-        def _():
+        @pl.when(place == levels - 1)
+        def _():
+            for shift in range(supers):
+                answer_copy(piece, shift).start()
+
+    @pl.when(place > 0)
+    def _():
+        forward_ref[...] = times_transposed(rhs[...], inverse_packed[...])
+
+    @pl.when(place == 0)
+    def _():
+        pack_products()
+
+    @pl.when(place < levels - 1)
+    def _():
+        rhs[...] = times(forward_ref[...], inverse_packed[...])
+        for piece in range(PIECES):
+            part = pl.ds(piece * rows, rows)
             for shift in range(supers):
                 pltpu.make_async_copy(
                     arrived[piece].at[shift], arrived[piece].at[shift], arrived_sem.at[piece, shift]
                 ).wait()
             picked = jnp.concatenate([arrived[piece][slot] for slot in slots], axis=1)
-            rhs[part, :] = rhs[part, :] - times(picked, factor_packed[...])
-
-        fresh = times(rhs[part, :], inverse_packed[...])
-        solved[piece] = fresh
-        answer_ref[part, :] = fresh
-
-        @pl.when(place > 0)
-        def _():
-            for shift in range(supers):
-                answer_copy(piece, shift).start()
+            fresh = rhs[part, :] - times(picked, packed[...])
+            solved[piece] = fresh
+            answer_ref[part, :] = fresh
+
+            @pl.when(place > 0)
+            def _():
+                for shift in range(supers):
+                    answer_copy(piece, shift).start()
 
     @pl.when(place < levels - 1)
     def _():
@@ -189,7 +228,7 @@
     loads, width = rhs.shape[2:]
     count = factor.shape[2]
     rows = loads // PIECES
-    block = jax.ShapeDtypeStruct((loads, width), jnp.float32)
+    block = pltpu.VMEM((loads, width), jnp.float32)
     anywhere = pl.BlockSpec(memory_space=pl.ANY)
     solved, answer = pl.pallas_call(
         functools.partial(kernel, levels, supers),

time: 40.7 us -> 36 us (0.88)
  Pallas kernels: 37.9 us -> 34 us
  local copies, waits for them, and re-layouts: 2 us -> 1.23 us
    pallas_call x1, Pallas kernels: 37.9 us -> 34 us  [body(): pl.pallas_call(functools.partial(kernel, levels, supers), out_shape=(bloc...]
    unnamed x4 -> x2, local copies, waits for them, and re-layouts: 2 us -> 1.23 us
where the time goes in v2:
time: 36 us; the launch traced here: 35.9 us
  Pallas kernels  34 us (94%)
  local copies, waits for them, and re-layouts  1.23 us (3%)
  between operations  0.64 us (2%)
    pallas_call x1, Pallas kernels, body(): pl.pallas_call(functools.partial(kernel, levels, supers), out_shape=(bloc...  34 us
    unnamed x2, local copies, waits for them, and re-layouts  1.23 us

profile of v2, /device:TPU:0, one launch (start us, length us, event | category | flops | bytes accessed | tf_op | source)
XLA Modules:
  0.0 35.9 jit_solution(15641940485401952453)
XLA Ops:
  0.6 34.0 %shard_map.59 = (f32[64,128]{1,0:T(8,128)S(1)}, f32[64,128]{1,0:T(8,128)S(1)}) custom-call(f32[64,128]{1,0:T(8,128)} %bitcast.9, f32[128,128]{1,0:T(8,128)} %bitcast.8, f32[8,128,128]{2,1,0:T(8,128)} %bitcast.7, s32[1,1,8]{2,1,0:T(1,128)} %pattern_hbm.1), custom_call_target="tpu_custom_call" | custom-call | tf_op jit(solution)/shard_map/pallas_call | solution.py:233
  34.6 0.6 %copy.8 = f32[1,1,64,128]{3,2,1,0:T(8,128)} copy(f32[1,1,64,128]{3,2,1,0:T(8,128)S(1)} %bitcast.6) | data formatting | bytes 65536
  35.2 0.6 %copy.9 = f32[1,1,64,128]{3,2,1,0:T(8,128)} copy(f32[1,1,64,128]{3,2,1,0:T(8,128)S(1)} %bitcast.5) | data formatting | bytes 65536

commit v3 on v2

--- a/solution.py
+++ b/solution.py
@@ -29,6 +29,16 @@
     return both[:rows] + both[rows:]
 
 
+def times_turned(value, turned):
+    rows = value.shape[0]
+    high, low = halves(value)
+    stacked = jnp.concatenate(
+        [jnp.concatenate([high, low], axis=1), jnp.concatenate([low, high], axis=1)], axis=0
+    )
+    both = jnp.dot(stacked, turned, preferred_element_type=jnp.float32)
+    return both[:rows] + both[rows:]
+
+
 def times(value, packed):
     rows = value.shape[0]
     width = packed.shape[1] // 2
@@ -41,10 +51,11 @@
 
 
 def kernel(
-    levels, supers, rhs_hbm, inverse_hbm, factor_hbm, pattern_hbm, forward_ref, answer_ref,
-    rhs, inverse, factor, pattern, inverse_packed, packed, terms, outbox, inbox, solved,
+    levels, supers, rhs_hbm, inverse_hbm, factor_hbm, pattern_hbm, both_ref,
+    rhs, inverse, factor, pattern, inverse_packed, packed, turned, terms, outbox, inbox, solved,
     load_sem, outbox_sem, inbox_sem, solved_sem, arrived_sem, *arrived,
 ):
+    forward_ref, answer_ref = both_ref.at[0], both_ref.at[1]
     place = lax.axis_index("chain")
     me = lax.axis_index("col")
     count, _, width = factor.shape
@@ -82,14 +93,20 @@
     inverse_packed[:, :width] = high
     inverse_packed[:, width:] = low
 
+    full = count == supers
+
     def pack(block, value):
         high, low = halves(value)
         packed[block * width:(block + 1) * width, :width] = high
         packed[block * width:(block + 1) * width, width:] = low
 
-    def pack_products():
-        for block in range(count):
-            pack(block, times(factor[block], inverse_packed[...]))
+    def pack_turned(block, value):
+        high, low = halves(value.T)
+        turned[:width, block * width:(block + 1) * width] = high
+        turned[width:, block * width:(block + 1) * width] = low
+
+    def block_of(block):
+        return factor[jnp.maximum(origin[block], 0)] if full else factor[block]
 
     loading[2].wait()
     loading[3].wait()
@@ -105,13 +122,16 @@
     @pl.when(place == 0)
     def _():
         for block in range(count):
-            pack(block, factor[block])
+            pack_turned(block, block_of(block))
         rhs[...] = times_transposed(rhs[...], inverse_packed[...])
         forward_ref[...] = rhs[...]
 
     @pl.when((place > 0) & (place < levels - 1))
     def _():
-        pack_products()
+        for block in range(count):
+            product = times(block_of(block), inverse_packed[...])
+            pack(block, product)
+            pack_turned(block, product)
 
     @pl.when(place == levels - 1)
     def _():
@@ -152,14 +172,16 @@
 
         @pl.when(place < levels - 1)
         def _():
-            wide = times_transposed(rhs[part, :], packed[...])
-            for block in range(count):
-                terms[block] = wide[:, block * width:(block + 1) * width]
-            for shift in range(supers):
-                picked = terms[jnp.maximum(origin[shift], 0)]
-                if count < supers:
-                    picked = jnp.where(origin[shift] >= 0, picked, 0.0)
-                outbox[piece, shift] = picked
+            wide = times_turned(rhs[part, :], turned[...])
+            if full:
+                for shift in range(supers):
+                    outbox[piece, shift] = wide[:, shift * width:(shift + 1) * width]
+            else:
+                for block in range(count):
+                    terms[block] = wide[:, block * width:(block + 1) * width]
+                for shift in range(supers):
+                    picked = terms[jnp.maximum(origin[shift], 0)]
+                    outbox[piece, shift] = jnp.where(origin[shift] >= 0, picked, 0.0)
 
         @pl.when(place == levels - 1)
         def _():
@@ -188,7 +210,8 @@
 
     @pl.when(place == 0)
     def _():
-        pack_products()
+        for block in range(count):
+            pack(block, times(block_of(block), inverse_packed[...]))
 
     @pl.when(place < levels - 1)
     def _():
@@ -199,7 +222,11 @@
                 pltpu.make_async_copy(
                     arrived[piece].at[shift], arrived[piece].at[shift], arrived_sem.at[piece, shift]
                 ).wait()
-            picked = jnp.concatenate([arrived[piece][slot] for slot in slots], axis=1)
+            if full:
+                chosen = [arrived[piece][(supers - shift) % supers] for shift in range(supers)]
+            else:
+                chosen = [arrived[piece][slot] for slot in slots]
+            picked = jnp.concatenate(chosen, axis=1)
             fresh = rhs[part, :] - times(picked, packed[...])
             solved[piece] = fresh
             answer_ref[part, :] = fresh
@@ -228,13 +255,13 @@
     loads, width = rhs.shape[2:]
     count = factor.shape[2]
     rows = loads // PIECES
-    block = pltpu.VMEM((loads, width), jnp.float32)
+    block = pltpu.VMEM((2, loads, width), jnp.float32)
     anywhere = pl.BlockSpec(memory_space=pl.ANY)
-    solved, answer = pl.pallas_call(
+    both = pl.pallas_call(
         functools.partial(kernel, levels, supers),
-        out_shape=(block, block),
+        out_shape=block,
         in_specs=[anywhere] * 4,
-        out_specs=[pl.BlockSpec(memory_space=pltpu.VMEM)] * 2,
+        out_specs=pl.BlockSpec(memory_space=pltpu.VMEM),
         scratch_shapes=[
             pltpu.VMEM((loads, width), jnp.float32),
             pltpu.VMEM((width, width), jnp.float32),
@@ -242,6 +269,7 @@
             pltpu.SMEM((1, 1, count), jnp.int32),
             pltpu.VMEM((width, 2 * width), jnp.bfloat16),
             pltpu.VMEM((count * width, 2 * width), jnp.bfloat16),
+            pltpu.VMEM((2 * width, count * width), jnp.bfloat16),
             pltpu.VMEM((count, rows, width), jnp.float32),
             pltpu.VMEM((PIECES, supers, rows, width), jnp.float32),
             pltpu.VMEM((PIECES, supers, rows, width), jnp.float32),
@@ -255,7 +283,7 @@
         ],
         compiler_params=pltpu.CompilerParams(collective_id=0, has_side_effects=True),
     )(rhs[0, 0], inverse[0, 0], factor[0, 0], pattern)
-    return (solved[None, None], answer[None, None])
+    return (both[None, :1], both[None, 1:])
 
 
 def solution(mesh):

time: 36 us -> 35.2 us (0.978)
  local copies, waits for them, and re-layouts: 1.23 us -> 0.63 us
    unnamed x2 -> x0, local copies, waits for them, and re-layouts: 1.23 us -> none
    broadcast_in_dim x0 -> x1, local copies, waits for them, and re-layouts: none -> 0.63 us  [body(): return (both[None, :1], both[None, 1:])]
where the time goes in v3:
time: 35.2 us; the launch traced here: 35 us
  Pallas kernels  33.8 us (96%)
  between operations  0.64 us (2%)
  local copies, waits for them, and re-layouts  0.63 us (2%)
    pallas_call x1, Pallas kernels, body(): pl.pallas_call(functools.partial(kernel, levels, supers), out_shape=block...  33.8 us

profile of v3, /device:TPU:0, one launch (start us, length us, event | category | flops | bytes accessed | tf_op | source)
XLA Modules:
  0.0 35.0 jit_solution(5311643299739409623)
XLA Ops:
  0.6 33.8 %shard_map.59 = f32[2,64,128]{2,1,0:T(8,128)S(1)} custom-call(f32[64,128]{1,0:T(8,128)} %bitcast.9, f32[128,128]{1,0:T(8,128)} %bitcast.8, f32[8,128,128]{2,1,0:T(8,128)} %bitcast.7, s32[1,1,8]{2,1,0:T(1,128)} %pattern_hbm.1), custom_call_target="tpu_custom_call" | custom-call | tf_op jit(solution)/shard_map/pallas_call | solution.py:260
  34.4 0.6 %slice_bitcast_fusion = (f32[1,1,64,128]{3,2,1,0:T(8,128)}, f32[1,1,64,128]{3,2,1,0:T(8,128)}) fusion(f32[2,64,128]{2,1,0:T(8,128)S(1)} %shard_map.59), kind=kLoop, calls=%fused_computation | loop fusion | bytes 131072 | tf_op jit(solution)/shard_map/broadcast_in_dim | solution.py:286

commit v4 on v3

--- a/solution.py
+++ b/solution.py
@@ -142,7 +142,7 @@
             src_ref=outbox.at[piece, shift],
             dst_ref=inbox.at[piece, shift],
             send_sem=outbox_sem.at[piece, shift],
-            recv_sem=inbox_sem.at[piece, shift],
+            recv_sem=inbox_sem.at[piece],
             device_id={"chain": place + 1, "col": peers[shift]},
             device_id_type=MESH,
         )
@@ -152,7 +152,7 @@
             src_ref=solved.at[piece],
             dst_ref=arrived[piece].at[shift],
             send_sem=solved_sem.at[piece, shift],
-            recv_sem=arrived_sem.at[piece, shift],
+            recv_sem=arrived_sem.at[piece],
             device_id={"chain": place - 1, "col": peers[shift]},
             device_id_type=MESH,
         )
@@ -162,12 +162,8 @@
 
         @pl.when(place > 0)
         def _():
-            total = rhs[part, :]
-            for shift in range(supers):
-                pltpu.make_async_copy(
-                    inbox.at[piece, shift], inbox.at[piece, shift], inbox_sem.at[piece, shift]
-                ).wait()
-                total = total - inbox[piece, shift]
+            pltpu.make_async_copy(inbox.at[piece], inbox.at[piece], inbox_sem.at[piece]).wait()
+            total = rhs[part, :] - jnp.sum(inbox[piece], axis=0)
             rhs[part, :] = total
 
         @pl.when(place < levels - 1)
@@ -218,10 +214,7 @@
         rhs[...] = times(forward_ref[...], inverse_packed[...])
         for piece in range(PIECES):
             part = pl.ds(piece * rows, rows)
-            for shift in range(supers):
-                pltpu.make_async_copy(
-                    arrived[piece].at[shift], arrived[piece].at[shift], arrived_sem.at[piece, shift]
-                ).wait()
+            pltpu.make_async_copy(arrived[piece], arrived[piece], arrived_sem.at[piece]).wait()
             if full:
                 chosen = [arrived[piece][(supers - shift) % supers] for shift in range(supers)]
             else:
@@ -276,9 +269,9 @@
             pltpu.VMEM((PIECES, rows, width), jnp.float32),
             pltpu.SemaphoreType.DMA((4,)),
             pltpu.SemaphoreType.DMA((PIECES, supers)),
+            pltpu.SemaphoreType.DMA((PIECES,)),
             pltpu.SemaphoreType.DMA((PIECES, supers)),
-            pltpu.SemaphoreType.DMA((PIECES, supers)),
-            pltpu.SemaphoreType.DMA((PIECES, supers)),
+            pltpu.SemaphoreType.DMA((PIECES,)),
             *[pltpu.VMEM((supers, rows, width), jnp.float32)] * PIECES,
         ],
         compiler_params=pltpu.CompilerParams(collective_id=0, has_side_effects=True),

time: 35.2 us -> 34.7 us (0.986)
  Pallas kernels: 33.8 us -> 33.3 us
    pallas_call x1, Pallas kernels: 33.8 us -> 33.3 us  [body(): pl.pallas_call(functools.partial(kernel, levels, supers), out_shape=block...]
where the time goes in v4:
time: 34.7 us; the launch traced here: 34.5 us
  Pallas kernels  33.3 us (96%)
  between operations  0.64 us (2%)
  local copies, waits for them, and re-layouts  0.63 us (2%)
    pallas_call x1, Pallas kernels, body(): pl.pallas_call(functools.partial(kernel, levels, supers), out_shape=block...  33.3 us

profile of v4, /device:TPU:0, one launch (start us, length us, event | category | flops | bytes accessed | tf_op | source)
XLA Modules:
  0.0 34.5 jit_solution(10891797575384116285)
XLA Ops:
  0.6 33.3 %shard_map.59 = f32[2,64,128]{2,1,0:T(8,128)S(1)} custom-call(f32[64,128]{1,0:T(8,128)} %bitcast.9, f32[128,128]{1,0:T(8,128)} %bitcast.8, f32[8,128,128]{2,1,0:T(8,128)} %bitcast.7, s32[1,1,8]{2,1,0:T(1,128)} %pattern_hbm.1), custom_call_target="tpu_custom_call" | custom-call | tf_op jit(solution)/shard_map/pallas_call | solution.py:253
  33.9 0.6 %slice_bitcast_fusion = (f32[1,1,64,128]{3,2,1,0:T(8,128)}, f32[1,1,64,128]{3,2,1,0:T(8,128)}) fusion(f32[2,64,128]{2,1,0:T(8,128)S(1)} %shard_map.59), kind=kLoop, calls=%fused_computation | loop fusion | bytes 131072 | tf_op jit(solution)/shard_map/broadcast_in_dim | solution.py:279
